TPU v7x, 256 devices: a whole 4x4x8 slice. The times are simulated.
256 devices in a mesh: dp: 4 (over x), space: 64 (over y, z, core).
Axes of the slice: x: 4, y: 4, z: 8, core: 2. Of those that a mesh axis runs over, the one named last changes fastest.
Arguments:
- features: bfloat16 [4, 64, 96, 1024], P('dp', 'space'), may hold values from -6 to 6
- cotangent: bfloat16 [4, 64, 192, 128], P('dp', 'space'), may hold values from -6 to 6
- conv_weight: bfloat16 [96, 2592], replicated, may hold values from -0.125 to 0.125
- down_weight: bfloat16 [192, 768], replicated, may hold values from -0.21875 to 0.21875
- neighbours: int32 [4, 64, 26], P('dp', 'space'), may hold values from -1 to 63, as said below
Outputs:
- coarse_out: bfloat16 [4, 64, 192, 128], P('dp', 'space')
- grad_features: float32 [4, 64, 96, 1024], P('dp', 'space')
- grad_conv: float32 [96, 2592], replicated
- grad_down: float32 [192, 768], replicated
Inputs may be any that keep to these rules, and one draw needn't show every extreme that they name: The blocks of a tile sit at distinct cells of a grid; if neighbours[t, s, d] = p is not -1 then neighbours[t, p, 25 - d] = s; a row never names its own block and names a device at most once.
All inputs are finite; a program needn't handle non-finite values.
Results may differ from a plain program's by a relative error of at most 0.0095.
Values may be sent and summed in bfloat16 or wider, within the bound.
No kernel may reach another device: no remote copies, remote signals or barrier semaphores. Data moves between devices by JAX's collectives and lax.ppermute only.
A program may use at most 128 MiB of HBM per device.

v0:
```python
import jax
import jax.numpy as jnp
from jax import lax
from jax.sharding import PartitionSpec as P

BRICK = 8
DIRECTIONS = [
    (step_x, step_y, step_z)
    for step_x in (-1, 0, 1)
    for step_y in (-1, 0, 1)
    for step_z in (-1, 0, 1)
    if (step_x, step_y, step_z) != (0, 0, 0)
]
EPSILON = 1e-06


def cut_inner(offset, extent):
    if offset < 0:
        return slice(0, 1)
    if offset > 0:
        return slice(extent - 1, extent)
    return slice(0, extent)


def cut_outer(offset, extent):
    if offset < 0:
        return slice(0, 1)
    if offset > 0:
        return slice(extent + 1, extent + 2)
    return slice(1, extent + 1)


def inner_layer(block_data, offset):
    return block_data[
        :,
        cut_inner(offset[0], block_data.shape[1]),
        cut_inner(offset[1], block_data.shape[2]),
        cut_inner(offset[2], block_data.shape[3]),
    ]


def outer_layer(padded, offset):
    return padded[
        :,
        cut_outer(offset[0], padded.shape[1] - 2),
        cut_outer(offset[1], padded.shape[2] - 2),
        cut_outer(offset[2], padded.shape[3] - 2),
    ]


def conv_taps(padded, weight_matrix):
    channels = padded.shape[0]
    size_x, size_y, size_z = (padded.shape[1] - 2, padded.shape[2] - 2, padded.shape[3] - 2)
    accumulated = jnp.zeros((weight_matrix.shape[0], size_x * size_y * size_z), jnp.float32)
    for step_x in range(3):
        for step_y in range(3):
            columns = jnp.concatenate(
                [
                    padded[
                        :,
                        step_x : step_x + size_x,
                        step_y : step_y + size_y,
                        step_z : step_z + size_z,
                    ]
                    for step_z in range(3)
                ],
                axis=0,
            ).reshape(3 * channels, size_x * size_y * size_z)
            start_col = (step_x * 3 + step_y) * 3 * channels
            accumulated = accumulated + jnp.dot(
                weight_matrix[:, start_col : start_col + 3 * channels],
                columns,
                preferred_element_type=jnp.float32,
            )
    return accumulated


def weight_taps(padded, grad_out):
    channels = padded.shape[0]
    size_x, size_y, size_z = (padded.shape[1] - 2, padded.shape[2] - 2, padded.shape[3] - 2)
    blocks_out = []
    for step_x in range(3):
        for step_y in range(3):
            columns = jnp.concatenate(
                [
                    padded[
                        :,
                        step_x : step_x + size_x,
                        step_y : step_y + size_y,
                        step_z : step_z + size_z,
                    ]
                    for step_z in range(3)
                ],
                axis=0,
            ).reshape(3 * channels, size_x * size_y * size_z)
            blocks_out.append(
                lax.dot_general(
                    grad_out, columns, (((1,), (1,)), ((), ())), preferred_element_type=jnp.float32
                )
            )
    return jnp.concatenate(blocks_out, axis=1)


def flipped(weight_matrix):
    channels = weight_matrix.shape[0]
    return (
        weight_matrix.reshape(channels, 27, channels)[:, ::-1, :]
        .transpose(2, 1, 0)
        .reshape(channels, 27 * channels)
    )


def coarse_patches(hidden_block):
    channels, size_x, size_y, size_z = hidden_block.shape
    split = hidden_block.reshape(channels, size_x // 2, 2, size_y // 2, 2, size_z // 2, 2)
    return split.transpose(2, 4, 6, 0, 1, 3, 5).reshape(
        8 * channels, size_x // 2 * (size_y // 2) * (size_z // 2)
    )


def from_patches(patch_data, channels, size_x, size_y, size_z):
    split = patch_data.reshape(2, 2, 2, channels, size_x // 2, size_y // 2, size_z // 2)
    return split.transpose(3, 4, 0, 5, 1, 6, 2).reshape(channels, size_x * size_y * size_z)


def silu_slope(activation):
    sigmoid_value = jax.nn.sigmoid(activation)
    return sigmoid_value * (1.0 + activation * (1.0 - sigmoid_value))


def normalized(accumulated):
    return accumulated * lax.rsqrt(jnp.mean(accumulated * accumulated) + EPSILON)


def shards(features, cotangent, conv_weight, down_weight, neighbours):
    channels = features.shape[2]
    block_side = BRICK
    block_depth = features.shape[3] // (block_side * block_side)
    peer_count = lax.axis_size("space")
    capacity = max(block_side * block_side, block_side * block_depth)
    owner_row = neighbours[0, 0]
    present = owner_row >= 0
    target = jnp.where(present, owner_row, peer_count)
    source = jnp.clip(owner_row, 0, peer_count - 1)

    def pack_faces(face_layers, wire_type):
        stacked = jnp.stack(
            [
                jnp.pad(
                    face_layer.reshape(channels, -1), ((0, 0), (0, capacity - face_layer[0].size))
                )
                for face_layer in face_layers
            ]
        )
        return (
            jnp.zeros((peer_count, channels, capacity), wire_type)
            .at[target]
            .set(stacked, mode="drop")
        )

    def unpack_faces(received, shapes):
        picked = jnp.take(received, source, axis=0) * present[:, None, None].astype(received.dtype)
        pieces = []
        for number, shape in enumerate(shapes):
            count = shape[1] * shape[2] * shape[3]
            pieces.append(picked[number, :, :count].reshape(shape))
        return pieces

    def fill_rim(block_data, received):
        padded = jnp.pad(block_data, ((0, 0), (1, 1), (1, 1), (1, 1)))
        pieces = unpack_faces(
            received, [inner_layer(block_data, offset).shape for offset in DIRECTIONS]
        )
        for offset, face_piece in zip(DIRECTIONS, pieces):
            padded = padded.at[
                :,
                cut_outer(offset[0], block_side),
                cut_outer(offset[1], block_side),
                cut_outer(offset[2], block_depth),
            ].set(face_piece)
        return padded

    own_block = features[0, 0].reshape(channels, block_side, block_side, block_depth)
    sent = pack_faces([inner_layer(own_block, offset) for offset in DIRECTIONS], jnp.bfloat16)
    received = lax.all_to_all(sent, "space", split_axis=0, concat_axis=0, tiled=True)
    padded = fill_rim(own_block, received)
    preact = conv_taps(padded, conv_weight)
    hidden = jax.nn.silu(preact).astype(jnp.bfloat16)
    patches = coarse_patches(hidden.reshape(channels, block_side, block_side, block_depth))
    coarse_out = jnp.dot(down_weight, patches, preferred_element_type=jnp.float32).astype(
        jnp.bfloat16
    )
    cot_block = cotangent[0, 0]
    down_part = lax.dot_general(
        cot_block, patches, (((1,), (1,)), ((), ())), preferred_element_type=jnp.float32
    )
    spread_back = from_patches(
        jnp.dot(down_weight.T, cot_block, preferred_element_type=jnp.float32),
        channels,
        block_side,
        block_side,
        block_depth,
    )
    grad_pre = (spread_back * silu_slope(preact)).astype(jnp.bfloat16)
    conv_part = weight_taps(padded, grad_pre)
    flip_weight = flipped(conv_weight)
    grad_block = grad_pre.reshape(channels, block_side, block_side, block_depth)
    widened = jnp.pad(grad_block, ((0, 0), (2, 2), (2, 2), (2, 2)))
    full_grad = conv_taps(widened, flip_weight).reshape(
        channels, block_side + 2, block_side + 2, block_depth + 2
    )
    spill_buffer = pack_faces(
        [outer_layer(full_grad, offset) for offset in DIRECTIONS], jnp.float32
    )
    got_spill = lax.all_to_all(
        spill_buffer.astype(jnp.bfloat16), "space", split_axis=0, concat_axis=0, tiled=True
    ).astype(spill_buffer.dtype)
    inner_part = full_grad[:, 1:-1, 1:-1, 1:-1]
    pieces = unpack_faces(
        got_spill, [inner_layer(inner_part, offset).shape for offset in DIRECTIONS]
    )
    for offset, face_piece in zip(DIRECTIONS, pieces):
        inner_part = inner_part.at[
            :,
            cut_inner(offset[0], block_side),
            cut_inner(offset[1], block_side),
            cut_inner(offset[2], block_depth),
        ].add(face_piece)
    grad_features = inner_part.reshape(channels, -1)
    conv_sum, down_sum = lax.psum((conv_part, down_part), ("dp", "space"))
    return (
        coarse_out[None, None],
        grad_features[None, None],
        normalized(conv_sum),
        normalized(down_sum),
    )


def solution(mesh):
    placed = (
        P("dp", "space", None, None),
        P("dp", "space", None, None),
        P(),
        P(),
        P("dp", "space", None),
    )
    return jax.shard_map(
        shards,
        mesh=mesh,
        in_specs=placed,
        out_specs=(P("dp", "space", None, None), P("dp", "space", None, None), P(), P()),
        check_vma=False,
    )
```

profile of v0, /device:TPU:2, one launch (start us, length us, event | category | flops | bytes accessed | tf_op | source)
XLA Modules:
  0.0 610.5 jit_solution(4286179501511224729)
XLA Ops:
  10.8 5.3 scatter_fusion
  16.1 12.1 %all-to-all-start = ((bf16[64,96,128]{2,1,0:T(8,128)(2,1)}), bf16[64,96,128]{2,1,0:T(8,128)(2,1)S(1)}, u32[]{:S(2)}, u32[]{:S(2)}) async-start(bf16[64,96,128]{2,1,0:T(8,128)(2,1)} %scatter_fusion), calls=%async_computation | async-start | bytes 3145728 | tf_op jit(solution)/shard_map/all_to_all | solution.py:185
  31.8 35.9 %all-to-all-done = bf16[64,96,128]{2,1,0:T(8,128)(2,1)S(1)} async-done(((bf16[64,96,128]{2,1,0:T(8,128)(2,1)}), bf16[64,96,128]{2,1,0:T(8,128)(2,1)S(1)}, u32[]{:S(2)}, u32[]{:S(2)}) %all-to-all-start) | async-done | bytes 1572896 | tf_op jit(solution)/shard_map/all_to_all | solution.py:185
  96.3 5.5 pad_slice_fusion.2
  105.8 2.4 pad_maximum_fusion.7
  110.1 2.4 pad_maximum_fusion.6
  114.4 2.4 pad_maximum_fusion.5
  118.7 2.4 pad_maximum_fusion.4
  123.0 2.4 pad_maximum_fusion.3
  127.2 2.6 pad_maximum_fusion.2
  131.7 2.4 pad_maximum_fusion.1
  135.9 2.4 pad_maximum_fusion
  154.9 3.7 scatter_fusion.1
  160.1 7.0 %all-to-all-start.1 = ((bf16[64,96,128]{2,1,0:T(8,128)(2,1)}), bf16[64,96,128]{2,1,0:T(8,128)(2,1)}, u32[]{:S(2)}, u32[]{:S(2)}) async-start(bf16[64,96,128]{2,1,0:T(8,128)(2,1)} %convert_element_type.100), calls=%async_computation.1 | async-start | bytes 3145728 | tf_op jit(solution)/shard_map/all_to_all | solution.py:215
  183.0 257.4 %all-reduce.49.cloned.1.call-done = (f32[96,2592]{1,0:T(8,128)}, f32[192,768]{1,0:T(8,128)}) async-done(((f32[96,2592]{1,0:T(8,128)}, f32[192,768]{1,0:T(8,128)}), (f32[96,2592]{1,0:T(8,128)}, f32[192,768]{1,0:T(8,128)})) %all-reduce.49.cloned.1.call-update) | async-done | bytes 1585168 | tf_op jit(solution)/shard_map/psum | solution.py:230
  448.8 3.5 convert_element_type.101
  452.3 3.6 gather_fusion.1
  469.1 2.6 scatter-add.91
  476.0 2.8 add_select_fusion.1
  478.8 4.6 scatter-add.95
  484.4 2.6 fusion.25
  491.7 3.0 scatter-add.101
  499.0 2.8 add_select_fusion
  501.8 4.8 scatter-add.105
  509.7 4.2 slice_add_fusion.1
  513.9 18.6 %scatter-add.106 = f32[96,8,8,16]{3,0,2,1:T(8,128)S(1)} dynamic-update-slice(f32[96,8,8,16]{3,0,2,1:T(8,128)S(1)} %scatter-add.105, f32[96,8,8,1]{3,0,2,1:T(8,128)} %slice_add_fusion.1, s32[]{:T(128)} %constant.1634.clone.1, s32[]{:T(128)} %constant.1634.clone.1, s32[]{:T(128)} %constant.1634.clone.1, s32[]{:T(128)} %constant.1634.clone.1) | dynamic-update-slice | bytes 49156 | tf_op jit(solution)/shard_map/scatter-add | solution.py:228
  534.9 4.4 slice_add_fusion
  539.3 23.3 %scatter-add.109 = f32[96,8,8,16]{3,0,2,1:T(8,128)S(1)} dynamic-update-slice(f32[96,8,8,16]{3,0,2,1:T(8,128)S(1)} %scatter-add.106, f32[96,8,8,1]{3,0,2,1:T(8,128)} %slice_add_fusion, s32[]{:T(128)} %constant.1634.clone.1, s32[]{:T(128)} %constant.1634.clone.1, s32[]{:T(128)} %constant.1634.clone.1, s32[]{:T(128)} %constant.1644.clone.1) | dynamic-update-slice | bytes 49156 | tf_op jit(solution)/shard_map/scatter-add | solution.py:228
  565.0 3.0 scatter-add.110
  573.9 3.6 scatter-add.114
  584.5 2.6 scatter-add.120
  592.9 3.3 scatter-add.124
  (355 shorter events, 153.4 us)
Async XLA Ops:
  16.1 12.3 %copy-start.22 = (bf16[192,768]{1,0:T(8,128)(2,1)S(1)}, bf16[192,768]{1,0:T(8,128)(2,1)}, u32[]{:S(2)}) copy-start(bf16[192,768]{1,0:T(8,128)(2,1)} %param.112) | copy-start | bytes 884740
  16.1 12.5 %copy-start.32 = (bf16[1,1,192,128]{3,2,1,0:T(8,128)(2,1)S(1)}, bf16[1,1,192,128]{3,2,1,0:T(8,128)(2,1)}, u32[]{:S(2)}) copy-start(bf16[1,1,192,128]{3,2,1,0:T(8,128)(2,1)} %param.110) | copy-start | bytes 147460
  16.1 51.6 %all-to-all-start = ((bf16[64,96,128]{2,1,0:T(8,128)(2,1)}), bf16[64,96,128]{2,1,0:T(8,128)(2,1)S(1)}, u32[]{:S(2)}, u32[]{:S(2)}) async-start(bf16[64,96,128]{2,1,0:T(8,128)(2,1)} %scatter_fusion), calls=%async_computation | async-start | bytes 3145728 | tf_op jit(solution)/shard_map/all_to_all | solution.py:185
  28.6 1.8 copy-start.19
  75.3 3.2 copy-start
  77.1 3.2 copy-start.2
  78.9 3.2 copy-start.4
  80.7 3.1 copy-start.6
  87.6 1.8 copy-start.30
  140.2 2.1 copy-start.14
  140.2 2.1 copy-start.18
  142.3 1.3 copy-start.13
  143.6 1.3 copy-start.12
  160.1 7.1 %copy-start.7 = (bf16[288,8,8,16]{0,3,2,1:T(8,128)(2,1)S(1)}, bf16[288,8,8,16]{0,3,2,1:T(8,128)(2,1)}, u32[]{:S(2)}) copy-start(bf16[288,8,8,16]{0,3,2,1:T(8,128)(2,1)} %copy-done.6) | copy-start | bytes 1769476
  160.1 8.0 %copy-start.31 = (bf16[96,1024]{1,0:T(8,128)(2,1)S(1)}, bf16[96,1024]{1,0:T(8,128)(2,1)}, u32[]{:S(2)}) copy-start(bf16[96,1024]{1,0:T(8,128)(2,1)} %get-tuple-element.737) | copy-start | bytes 589828
  160.1 288.7 %all-to-all-start.1 = ((bf16[64,96,128]{2,1,0:T(8,128)(2,1)}), bf16[64,96,128]{2,1,0:T(8,128)(2,1)}, u32[]{:S(2)}, u32[]{:S(2)}) async-start(bf16[64,96,128]{2,1,0:T(8,128)(2,1)} %convert_element_type.100), calls=%async_computation.1 | async-start | bytes 3145728 | tf_op jit(solution)/shard_map/all_to_all | solution.py:215
  167.1 1.7 copy-start.5
  167.1 2.7 copy-start.3
  167.1 273.4 %all-reduce.49.cloned.1.call-start = ((), (), s32[]{:S(2)}) async-start(), calls=%async_computation.2 | async-start | bytes 3244032 | tf_op jit(solution)/shard_map/psum | solution.py:230
  168.3 1.8 copy-start.1
  168.8 1.6 copy-start.23
  168.8 1.6 copy-start.24
  168.8 1.6 copy-start.25
  168.8 1.6 copy-start.26
  168.8 1.6 copy-start.27
  170.1 2.0 copy-start.33
  172.1 2.3 copy-start.36
  172.1 3.1 copy-start.37
  172.1 3.1 copy-start.38
  445.8 2.0 copy-start.16
  513.9 18.6 %copy-start.35 = (f32[1,96,64]{2,1,0:T(8,128)S(1)}, f32[1,96,64]{2,1,0:T(8,128)}, u32[]{:S(2)}) copy-start(f32[1,96,64]{2,1,0:T(8,128)} %get-tuple-element.662) | copy-start | bytes 73732
  539.3 23.3 %copy-start.34 = (f32[96,8,1,1]{1,0,3,2:T(8,128)S(1)}, f32[96,8,1,1]{1,0,3,2:T(8,128)}, u32[]{:S(2)}) copy-start(f32[96,8,1,1]{1,0,3,2:T(8,128)} %get-tuple-element.653) | copy-start | bytes 9220
  (11 other events, 12.5 us)
Sparse Core Ops, SparseCore 0:
  174.0 266.4 all-reduce.48
where the time goes:
time: 620 us; the launch traced here: 610 us
  waiting for transfers between devices  293 us (47%)
  local copies, waits for them, and re-layouts  177 us (29%)
  other arithmetic  73.2 us (12%)
  matrix products  29.7 us (5%)
  starting transfers between devices  19.2 us (3%)
  between operations  17.5 us (3%)
    psum x1, waiting for transfers between devices, shards(): conv_sum, down_sum = lax.psum((conv_part, down_part), ('dp', 'space'))  257 us
    scatter-add x22, local copies, waits for them, and re-layouts, shards(): inner_part = inner_part.at[:, cut_inner(offset[0], block_side), cut_inner...  75.3 us
    all_to_all x1, waiting for transfers between devices, shards(): lax.all_to_all(sent, 'space', split_axis=0, concat_axis=0, tiled=True)  35.9 us
    another operation x33, local copies, waits for them, and re-layouts  26 us
    concatenate x18, other arithmetic, conv_taps(): jnp.concatenate([padded[:, step_x:step_x + size_x, step_y:step_y + size_y...  24 us
    add x19, other arithmetic, shards(): inner_part = inner_part.at[:, cut_inner(offset[0], block_side), cut_inner...  22.2 us
    dot_general x18, matrix products, conv_taps(): jnp.dot(weight_matrix[:, start_col:start_col + 3 * channels], columns, pr...  19.3 us
    reshape x9, local copies, waits for them, and re-layouts, conv_taps(): columns = jnp.concatenate([padded[:, step_x:step_x + size_x, step_y:step_...  15.8 us
  transfers between devices with their start and end apart: 3, of which 2 were waited for; matrix products, arithmetic and copies ran while one was open for 4% of the time, Pallas kernels for 0%

commit v1 on v0

--- a/solution.py
+++ b/solution.py
@@ -2,6 +2,7 @@
 import jax.numpy as jnp
 from jax import lax
 from jax.sharding import PartitionSpec as P
+from jax.lax import psum
 
 BRICK = 8
 DIRECTIONS = [
@@ -12,6 +13,12 @@
     if (step_x, step_y, step_z) != (0, 0, 0)
 ]
 EPSILON = 1e-06
+
+
+def solve_positions_by_axis(mine_x):
+    back = psum(mine_x, axis_name="dp")
+    part_now = psum(back, "space")
+    return part_now
 
 
 def cut_inner(offset, extent):
@@ -227,7 +234,7 @@
             cut_inner(offset[2], block_depth),
         ].add(face_piece)
     grad_features = inner_part.reshape(channels, -1)
-    conv_sum, down_sum = lax.psum((conv_part, down_part), ("dp", "space"))
+    conv_sum, down_sum = solve_positions_by_axis((conv_part, down_part))
     return (
         coarse_out[None, None],
         grad_features[None, None],

time: 620 us -> 590 us (0.952)
  waiting for transfers between devices: 293 us -> 255 us
  local copies, waits for them, and re-layouts: 177 us -> 184 us
    psum x1 -> x2, waiting for transfers between devices: 257 us -> 220 us  [the longest x1 183 us: solve_positions_by_axis(): part_now = psum(back, 'space')]
    unnamed x141 -> x171, local copies, waits for them, and re-layouts: 14.3 us -> 15.2 us
  transfers between devices with their start and end apart: 3 -> 4, of which waited for: 2 -> 3; matrix products, arithmetic and copies ran while one was open for 4% -> 5% of each run, Pallas kernels for 0% -> 0%
where the time goes in v1:
time: 590 us; the launch traced here: 580 us
  waiting for transfers between devices  255 us (43%)
  local copies, waits for them, and re-layouts  184 us (31%)
  other arithmetic  74.2 us (13%)
  matrix products  30 us (5%)
  starting transfers between devices  19 us (3%)
  between operations  17.6 us (3%)
    psum x1, waiting for transfers between devices, solve_positions_by_axis(): part_now = psum(back, 'space')  183 us
    scatter-add x22, local copies, waits for them, and re-layouts, shards(): inner_part = inner_part.at[:, cut_inner(offset[0], block_side), cut_inner...  75.3 us
    psum x1, waiting for transfers between devices, solve_positions_by_axis(): back = psum(mine_x, axis_name='dp')  37.4 us
    all_to_all x1, waiting for transfers between devices, shards(): lax.all_to_all(sent, 'space', split_axis=0, concat_axis=0, tiled=True)  35.3 us
    another operation x33, local copies, waits for them, and re-layouts  26.1 us
    concatenate x18, other arithmetic, conv_taps(): jnp.concatenate([padded[:, step_x:step_x + size_x, step_y:step_y + size_y...  24 us
    add x19, other arithmetic, shards(): inner_part = inner_part.at[:, cut_inner(offset[0], block_side), cut_inner...  22.2 us
    dot_general x18, matrix products, conv_taps(): jnp.dot(weight_matrix[:, start_col:start_col + 3 * channels], columns, pr...  18.9 us
  transfers between devices with their start and end apart: 4, of which 3 were waited for; matrix products, arithmetic and copies ran while one was open for 5% of the time, Pallas kernels for 0%

profile of v1, /device:TPU:2, one launch (start us, length us, event | category | flops | bytes accessed | tf_op | source)
XLA Modules:
  0.0 580.2 jit_solution(2611429841952977329)
XLA Ops:
  10.8 5.3 scatter_fusion
  16.1 12.1 %all-to-all-start = ((bf16[64,96,128]{2,1,0:T(8,128)(2,1)}), bf16[64,96,128]{2,1,0:T(8,128)(2,1)S(1)}, u32[]{:S(2)}, u32[]{:S(2)}) async-start(bf16[64,96,128]{2,1,0:T(8,128)(2,1)} %scatter_fusion), calls=%async_computation | async-start | bytes 3145728 | tf_op jit(solution)/shard_map/all_to_all | solution.py:192
  32.4 35.3 %all-to-all-done = bf16[64,96,128]{2,1,0:T(8,128)(2,1)S(1)} async-done(((bf16[64,96,128]{2,1,0:T(8,128)(2,1)}), bf16[64,96,128]{2,1,0:T(8,128)(2,1)S(1)}, u32[]{:S(2)}, u32[]{:S(2)}) %all-to-all-start) | async-done | bytes 1572896 | tf_op jit(solution)/shard_map/all_to_all | solution.py:192
  99.0 5.5 pad_slice_fusion.2
  108.5 2.4 pad_maximum_fusion.7
  112.8 2.4 pad_maximum_fusion.6
  117.1 2.4 pad_maximum_fusion.5
  125.7 2.4 pad_maximum_fusion.3
  130.0 2.6 pad_maximum_fusion.2
  134.4 2.4 pad_maximum_fusion.1
  138.7 2.4 pad_maximum_fusion
  167.5 3.9 scatter_fusion.1
  172.8 6.8 %all-to-all-start.1 = ((bf16[64,96,128]{2,1,0:T(8,128)(2,1)}), bf16[64,96,128]{2,1,0:T(8,128)(2,1)}, u32[]{:S(2)}, u32[]{:S(2)}) async-start(bf16[64,96,128]{2,1,0:T(8,128)(2,1)} %convert_element_type.100), calls=%async_computation.1 | async-start | bytes 3145728 | tf_op jit(solution)/shard_map/all_to_all | solution.py:222
  179.7 37.4 %all-reduce.53.cloned.1.call-done = (f32[96,2592]{1,0:T(8,128)}, f32[192,768]{1,0:T(8,128)}) async-done(((f32[96,2592]{1,0:T(8,128)}, f32[192,768]{1,0:T(8,128)}), (f32[96,2592]{1,0:T(8,128)}, f32[192,768]{1,0:T(8,128)})) %all-reduce.53.cloned.1.call-update) | async-done | bytes 1585168 | tf_op jit(solution)/shard_map/psum | solution.py:19
  227.1 182.6 %all-reduce.51.cloned.1.call-done = (f32[96,2592]{1,0:T(8,128)}, f32[192,768]{1,0:T(8,128)}) async-done(((f32[96,2592]{1,0:T(8,128)}, f32[192,768]{1,0:T(8,128)}), (f32[96,2592]{1,0:T(8,128)}, f32[192,768]{1,0:T(8,128)})) %all-reduce.51.cloned.1.call-update) | async-done | bytes 1585168 | tf_op jit(solution)/shard_map/psum | solution.py:20
  418.1 3.5 convert_element_type.101
  421.6 3.7 gather_fusion.1
  438.6 2.6 scatter-add.91
  445.5 2.9 add_select_fusion.1
  448.4 4.7 scatter-add.95
  454.1 2.8 fusion.25
  461.3 3.2 scatter-add.101
  468.9 2.9 add_select_fusion
  471.7 4.9 scatter-add.105
  479.8 4.2 slice_add_fusion.1
  483.9 18.6 %scatter-add.106 = f32[96,8,8,16]{3,0,2,1:T(8,128)S(1)} dynamic-update-slice(f32[96,8,8,16]{3,0,2,1:T(8,128)S(1)} %scatter-add.105, f32[96,8,8,1]{3,0,2,1:T(8,128)} %slice_add_fusion.1, s32[]{:T(128)} %constant.1634.clone.1, s32[]{:T(128)} %constant.1634.clone.1, s32[]{:T(128)} %constant.1634.clone.1, s32[]{:T(128)} %constant.1634.clone.1) | dynamic-update-slice | bytes 49156 | tf_op jit(solution)/shard_map/scatter-add | solution.py:235
  504.9 4.5 slice_add_fusion
  509.4 23.3 %scatter-add.109 = f32[96,8,8,16]{3,0,2,1:T(8,128)S(1)} dynamic-update-slice(f32[96,8,8,16]{3,0,2,1:T(8,128)S(1)} %scatter-add.106, f32[96,8,8,1]{3,0,2,1:T(8,128)} %slice_add_fusion, s32[]{:T(128)} %constant.1634.clone.1, s32[]{:T(128)} %constant.1634.clone.1, s32[]{:T(128)} %constant.1634.clone.1, s32[]{:T(128)} %constant.1644.clone.1) | dynamic-update-slice | bytes 49156 | tf_op jit(solution)/shard_map/scatter-add | solution.py:235
  535.1 3.0 scatter-add.110
  543.9 3.6 scatter-add.114
  554.3 2.6 scatter-add.120
  562.7 3.3 scatter-add.124
  (388 shorter events, 162.5 us)
Async XLA Ops:
  9.4 6.7 %copy-start.40 = (s32[26]{0:T(128)}, s32[26]{0:T(128)S(1)}, u32[]{:S(2)}) copy-start(s32[26]{0:T(128)S(1)} %get-tuple-element.800) | copy-start | bytes 316
  16.1 12.3 %copy-start.14 = (bf16[192,768]{1,0:T(8,128)(2,1)S(1)}, bf16[192,768]{1,0:T(8,128)(2,1)}, u32[]{:S(2)}) copy-start(bf16[192,768]{1,0:T(8,128)(2,1)} %param.112) | copy-start | bytes 884740
  16.1 12.5 %copy-start.20 = (bf16[1,1,192,128]{3,2,1,0:T(8,128)(2,1)S(1)}, bf16[1,1,192,128]{3,2,1,0:T(8,128)(2,1)}, u32[]{:S(2)}) copy-start(bf16[1,1,192,128]{3,2,1,0:T(8,128)(2,1)} %param.110) | copy-start | bytes 147460
  16.1 51.6 %all-to-all-start = ((bf16[64,96,128]{2,1,0:T(8,128)(2,1)}), bf16[64,96,128]{2,1,0:T(8,128)(2,1)S(1)}, u32[]{:S(2)}, u32[]{:S(2)}) async-start(bf16[64,96,128]{2,1,0:T(8,128)(2,1)} %scatter_fusion), calls=%async_computation | async-start | bytes 3145728 | tf_op jit(solution)/shard_map/all_to_all | solution.py:192
  28.2 188.9 %all-reduce.53.cloned.1.call-start = ((), (), s32[]{:S(2)}) async-start(), calls=%async_computation.3 | async-start | bytes 3244032 | tf_op jit(solution)/shard_map/psum | solution.py:19
  28.6 1.8 copy-start.11
  31.8 36.9 %copy-start.37 = (s32[1024]{0:T(1024)}, s32[1024]{0:T(1024)S(1)}, u32[]{:S(2)}) copy-start(s32[1024]{0:T(1024)S(1)} %pad_clamp_fusion) | copy-start | bytes 12292
  31.9 36.9 %copy-start.38 = (pred[26]{0:T(512)(128)(4,1)}, pred[26]{0:T(512)(128)(4,1)S(1)}, u32[]{:S(2)}) copy-start(pred[26]{0:T(512)(128)(4,1)S(1)} %compare_and_fusion) | copy-start | bytes 82
  87.1 1.8 copy-start.16
  143.0 2.1 copy-start.6
  143.0 2.1 copy-start.10
  145.1 1.3 copy-start.5
  146.4 1.3 copy-start.4
  147.8 1.3 copy-start.3
  149.1 1.3 copy-start.2
  150.5 1.3 copy-start.1
  151.8 1.3 copy-start
  154.6 4.5 copy-start.19
  154.6 5.2 copy-start.21
  154.7 9.1 %copy-start.9 = (f32[96,10,10,18]{0,3,2,1:T(8,128)}, f32[96,10,10,18]{0,3,2,1:T(8,128)S(1)}, u32[]{:S(2)}) copy-start(f32[96,10,10,18]{0,3,2,1:T(8,128)S(1)} %reshape.2481) | copy-start | bytes 2073604
  154.7 6.8 %copy-start.15 = (f32[96,288]{1,0:T(8,128)S(1)}, f32[96,288]{1,0:T(8,128)}, u32[]{:S(2)}) copy-start(f32[96,288]{1,0:T(8,128)} %fusion.71) | copy-start | bytes 331780
  172.8 45.6 %copy-start.51 = (s32[4]{0:T(128)S(1)}, s32[4]{0:T(128)}, u32[]{:S(2)}) copy-start(s32[4]{0:T(128)} %constant.1649.clone.1) | copy-start | bytes 52
  172.8 46.3 %copy-start.52 = (s32[4]{0:T(128)S(1)}, s32[4]{0:T(128)}, u32[]{:S(2)}) copy-start(s32[4]{0:T(128)} %constant.1646.clone.1) | copy-start | bytes 52
  172.8 46.3 %copy-start.53 = (s32[4]{0:T(128)S(1)}, s32[4]{0:T(128)}, u32[]{:S(2)}) copy-start(s32[4]{0:T(128)} %constant.1650.clone.1) | copy-start | bytes 52
  172.8 245.2 %all-to-all-start.1 = ((bf16[64,96,128]{2,1,0:T(8,128)(2,1)}), bf16[64,96,128]{2,1,0:T(8,128)(2,1)}, u32[]{:S(2)}, u32[]{:S(2)}) async-start(bf16[64,96,128]{2,1,0:T(8,128)(2,1)} %convert_element_type.100), calls=%async_computation.1 | async-start | bytes 3145728 | tf_op jit(solution)/shard_map/all_to_all | solution.py:222
  179.6 43.6 %copy-start.42 = (f32[96,1,1,1]{0,3,2,1:T(1,128)S(1)}, f32[96,1,1,1]{0,3,2,1:T(1,128)}, u32[]{:S(2)}) copy-start(f32[96,1,1,1]{0,3,2,1:T(1,128)} %get-tuple-element.667) | copy-start | bytes 1156
  179.6 230.1 %all-reduce.51.cloned.1.call-start = ((), (), s32[]{:S(2)}) async-start(), calls=%async_computation.2 | async-start | bytes 3244032 | tf_op jit(solution)/shard_map/psum | solution.py:20
  415.0 2.0 copy-start.8
  421.6 3.7 copy-start.39
  421.6 3.7 copy-start.50
  483.9 18.6 %copy-start.23 = (f32[1,96,64]{2,1,0:T(8,128)S(1)}, f32[1,96,64]{2,1,0:T(8,128)}, u32[]{:S(2)}) copy-start(f32[1,96,64]{2,1,0:T(8,128)} %get-tuple-element.664) | copy-start | bytes 73732
  509.4 23.3 %copy-start.22 = (f32[96,8,1,1]{1,0,3,2:T(8,128)S(1)}, f32[96,8,1,1]{1,0,3,2:T(8,128)}, u32[]{:S(2)}) copy-start(f32[96,8,1,1]{1,0,3,2:T(8,128)} %get-tuple-element.655) | copy-start | bytes 9220
  (27 other events, 29.0 us)
Sparse Core Ops, SparseCore 0:
  164.1 52.8 all-reduce.52
  221.0 188.6 all-reduce.50
